TPU v7x, 256 devices: a whole 4x4x8 slice. The times are simulated.
256 devices in a mesh: lat: 4 (over x), lon: 2 (over core), ens: 32 (over z, y).
Axes of the slice: x: 4, y: 4, z: 8, core: 2. Of those that a mesh axis runs over, the one named last changes fastest.
Arguments:
- inputs: bfloat16 [32, 8, 1440, 256], P('ens', 'lat', 'lon'), may hold values from -12 to 12
- weight: bfloat16 [9, 256, 256], replicated, may hold values from -0.125 to 0.125
- spread: int32 [8], P('lat'), may hold values from 2 to 16, as said below
- target: bfloat16 [8, 1440, 256], P('lat', 'lon'), may hold values from -6 to 6
Outputs:
- response: bfloat16 [32, 8, 1440, 256], P('ens', 'lat', 'lon')
- grad_input: bfloat16 [32, 8, 1440, 256], P('ens', 'lat', 'lon')
- grad_weight: float32 [9, 256, 256], replicated
- loss: float32 [], replicated
Inputs may be any that keep to these rules, and one draw needn't show every extreme that they name: The filter of row o spans 2 spread[o] + 1 longitudes; spread is 16 on the 2 polar rows at each pole, which ignore it, and on the next row toward the equator.
All inputs are finite; a program needn't handle non-finite values.
Results may differ from a plain program's by a relative error of at most 0.009.
Values may be sent and summed in bfloat16 or wider, within the bound.
No kernel may reach another device: no remote copies, remote signals or barrier semaphores. Data moves between devices by JAX's collectives and lax.ppermute only.
A program may use at most 128 MiB of HBM per device.

v0:
```python
import math
import jax
import jax.numpy as jnp
from jax import lax
from jax.sharding import PartitionSpec as P

PCAP = 2
HMAX = 16
highest = lax.Precision.HIGHEST


def extended_2(block, sides, width):
    for axis, dim in sides:
        count = lax.axis_size(axis)
        forward = [(i, i + 1) for i in range(count - 1)]
        backward = [(target, source) for source, target in forward]
        low = lax.ppermute(
            lax.slice_in_dim(block, block.shape[dim] - width, None, axis=dim), axis, forward
        )
        high = lax.ppermute(lax.slice_in_dim(block, 0, width, axis=dim), axis, backward)
        block = jnp.concatenate([low, block, high], axis=dim)
    return block


def kernel_rows(spread_rows, lon_count, reach):
    halves = spread_rows.astype(jnp.float32)[:, None, None, None] / 2.0
    columns = jnp.arange(lon_count)
    window_cols = jnp.arange(lon_count + 2 * reach)
    offsets = (window_cols[None, :] - reach - columns[:, None]).astype(jnp.float32)
    centres = (jnp.arange(3) - 1).astype(jnp.float32)[None, :, None, None] * halves
    values = jnp.maximum(0.0, 1.0 - jnp.abs(offsets[None, None] - centres) / halves) / halves
    return values.astype(jnp.bfloat16)


def circle_basis(first_col, lon_count, circle):
    angles = 2.0 * math.pi * (first_col + jnp.arange(lon_count)).astype(jnp.float32) / circle
    return jnp.stack([jnp.ones_like(angles), jnp.cos(angles), jnp.sin(angles)])


def circular(circle_sums, basis, circle, row_count):
    cos_wave = basis[1][None, None, :, None]
    sin_wave = basis[2][None, None, :, None]
    pieces = []
    for lat_tap in range(3):
        tap_sums = circle_sums[:, :, lat_tap : lat_tap + row_count]
        mean_part = tap_sums[:, 0][:, :, None, :] / circle
        cosine_part = (
            2.0
            / circle
            * (cos_wave * tap_sums[:, 1][:, :, None, :] + sin_wave * tap_sums[:, 2][:, :, None, :])
        )
        sine_part = (
            2.0
            / circle
            * (cos_wave * tap_sums[:, 2][:, :, None, :] - sin_wave * tap_sums[:, 1][:, :, None, :])
        )
        pieces += [jnp.broadcast_to(mean_part, cosine_part.shape), cosine_part, sine_part]
    return jnp.stack(pieces, 2)


def crps_terms(values, every_member, truth, lat_weight, member_total):
    miss = values - truth
    own_dist = jnp.sqrt(miss * miss + 0.25)
    own_slope = miss / own_dist

    def add_member(member, carry):
        pair_dist, pair_slope = carry
        other = lax.dynamic_index_in_dim(every_member, member, 0, keepdims=True).astype(jnp.float32)
        gap_value = values - other
        distance = jnp.sqrt(gap_value * gap_value + 0.25)
        return (pair_dist + distance, pair_slope + gap_value / distance)

    start = (jnp.zeros_like(values), jnp.zeros_like(values))
    pair_dist, pair_slope = lax.fori_loop(0, member_total, add_member, start)
    pair_dist = pair_dist - 0.5
    scores = own_dist / member_total - pair_dist / (2 * member_total * (member_total - 1))
    weighted = jnp.sum(lat_weight * scores)
    slopes = (
        lat_weight * (own_slope / member_total - pair_slope / (member_total * (member_total - 1)))
    ).astype(jnp.bfloat16)
    return (weighted, slopes)


def per_device(inputs, weight, spread, target):
    ens_local, row_count, lon_count, channels = inputs.shape
    reach = HMAX
    lat_total = row_count * lax.axis_size("lat")
    lon_total = lon_count * lax.axis_size("lon")
    lon_first = lax.axis_index("lon") * lon_count
    global_rows = lax.axis_index("lat") * row_count + jnp.arange(row_count)
    polar_rows = (global_rows < PCAP) | (global_rows >= lat_total - PCAP)
    polar_mask = polar_rows[None, :, None, None, None]
    kernels = kernel_rows(spread, lon_count, reach)
    local_basis = circle_basis(lon_first, lon_count, lon_total)
    extended = extended_2(inputs, (("lat", 1),), 1)
    whole_circle = lax.all_gather(extended, "lon", axis=2, tiled=True)
    window_start = (lon_first - reach + lon_total) % lon_total
    doubled = jnp.concatenate([whole_circle, whole_circle], 2)
    window = lax.dynamic_slice_in_dim(doubled, window_start, lon_count + 2 * reach, 2)
    full_basis = circle_basis(0, lon_total, lon_total)
    circle_sums = jnp.einsum(
        "pj,erjc->eprc", full_basis, whole_circle.astype(jnp.float32), precision=highest
    )
    banded = jnp.concatenate(
        [
            jnp.einsum(
                "objq,eoqc->eobjc",
                kernels,
                window[:, lat_tap : lat_tap + row_count],
                preferred_element_type=jnp.float32,
            )
            for lat_tap in range(3)
        ],
        2,
    )
    rounds = circular(circle_sums, local_basis, lon_total, row_count)
    features = jnp.where(polar_mask, rounds, banded).astype(jnp.bfloat16)
    response = jnp.einsum(
        "eokjc,kcd->eojd", features, weight, preferred_element_type=jnp.float32
    ).astype(jnp.bfloat16)
    member_total = ens_local * lax.axis_size("ens")
    row_weight = jnp.sin(math.pi * (global_rows.astype(jnp.float32) + 0.5) / lat_total)
    ensemble = lax.all_gather(response, "ens", axis=0, tiled=True)
    truth = target.astype(jnp.float32)[None]
    weighted, slopes = crps_terms(
        response.astype(jnp.float32), ensemble, truth, row_weight[None, :, None, None], member_total
    )
    loss_part = weighted / (lat_total * lon_total * channels)
    weight_part = jnp.einsum(
        "eokjc,eojd->kcd", features, slopes, preferred_element_type=jnp.float32
    )
    weight_sum, loss = lax.psum((weight_part, loss_part), ("lat", "lon", "ens"))
    grad_weight = weight_sum * math.sqrt(weight.shape[0] * channels) / (lat_total * lon_total)
    feature_grad = jnp.einsum(
        "eojd,kcd->eokjc", slopes, weight, preferred_element_type=jnp.float32
    ).astype(jnp.bfloat16)
    zero_grad = jnp.zeros_like(feature_grad)
    band_grad = jnp.where(polar_mask, zero_grad, feature_grad)
    circle_grad = jnp.where(polar_mask, feature_grad, zero_grad)
    window_grad = jnp.zeros(
        (ens_local, row_count + 2, lon_count + 2 * reach, channels), jnp.float32
    )
    sum_grad = jnp.zeros((ens_local, 3, row_count + 2, channels), jnp.float32)
    cos_wave = local_basis[1]
    sin_wave = local_basis[2]
    for lat_tap in range(3):
        picked = band_grad[:, :, 3 * lat_tap : 3 * lat_tap + 3]
        window_grad = window_grad.at[:, lat_tap : lat_tap + row_count].add(
            jnp.einsum("objq,eobjc->eoqc", kernels, picked, preferred_element_type=jnp.float32)
        )
        tap_grad = circle_grad[:, :, 3 * lat_tap : 3 * lat_tap + 3].astype(jnp.float32)
        mean_grad = jnp.sum(tap_grad[:, :, 0], axis=2) / lon_total
        cos_grad = (
            2.0
            / lon_total
            * (
                jnp.einsum("j,eojc->eoc", cos_wave, tap_grad[:, :, 1], precision=highest)
                - jnp.einsum("j,eojc->eoc", sin_wave, tap_grad[:, :, 2], precision=highest)
            )
        )
        sin_grad = (
            2.0
            / lon_total
            * (
                jnp.einsum("j,eojc->eoc", sin_wave, tap_grad[:, :, 1], precision=highest)
                + jnp.einsum("j,eojc->eoc", cos_wave, tap_grad[:, :, 2], precision=highest)
            )
        )
        sum_grad = sum_grad.at[:, :, lat_tap : lat_tap + row_count].add(
            jnp.stack([mean_grad, cos_grad, sin_grad], 1)
        )
    spread_back = jnp.einsum("pj,eprc->erjc", full_basis, sum_grad, precision=highest)
    placed = jnp.zeros((ens_local, row_count + 2, 2 * lon_total, channels), jnp.float32)
    placed = lax.dynamic_update_slice_in_dim(placed, window_grad, window_start, 2)
    spread_back = spread_back + placed[:, :, :lon_total] + placed[:, :, lon_total:]
    core = lax.psum_scatter(
        spread_back.astype(jnp.bfloat16), "lon", scatter_dimension=2, tiled=True
    ).astype(jnp.float32)
    edges = jnp.concatenate([core[:, :1], core[:, row_count + 1 :]], 1)
    arrived_rows = extended_2(edges.astype(jnp.bfloat16), (("lat", 1),), 1).astype(edges.dtype)
    inner = core[:, 1 : row_count + 1]
    inner = inner.at[:, 0].add(arrived_rows[:, 0])
    inner = inner.at[:, row_count - 1].add(arrived_rows[:, 3])
    return (response, inner.astype(jnp.bfloat16), grad_weight, loss)


def solution(mesh):
    in_specs = (P("ens", "lat", "lon", None), P(), P("lat"), P("lat", "lon", None))
    out_specs = (P("ens", "lat", "lon", None), P("ens", "lat", "lon", None), P(), P())
    return jax.shard_map(
        per_device, mesh=mesh, in_specs=in_specs, out_specs=out_specs, check_vma=False
    )
```

profile of v0, /device:TPU:2, one launch (start us, length us, event | category | flops | bytes accessed | tf_op | source)
XLA Modules:
  0.0 740.7 jit_solution(5865980801284775677)
XLA Ops:
  14.4 6.3 collective-permute-done
  27.0 19.3 %all-gather.4.cloned.1.call-done = bf16[1,4,1440,256]{3,2,1,0:T(8,128)(2,1)} async-done(((bf16[1,4,720,256]{3,2,1,0:T(8,128)(2,1)}), bf16[1,4,1440,256]{3,2,1,0:T(8,128)(2,1)}) %all-gather.4.cloned.1.call-update) | async-done | bytes 2949136 | tf_op jit(solution)/shard_map/all_gather | solution.py:96
  71.5 174.4 %all-gather.6.cloned.1.call-done = bf16[64,720,256]{2,1,0:T(8,128)(2,1)} async-done(((bf16[2,720,256]{2,1,0:T(8,128)(2,1)}), bf16[64,720,256]{2,1,0:T(8,128)(2,1)}) %all-gather.6.cloned.1.call-update) | async-done | bytes 23592976 | tf_op jit(solution)/shard_map/all_gather | solution.py:123
  245.9 140.6 %while.24 = (s32[]{:T(128)}, f32[1,2,720,256]{3,2,1,0:T(8,128)}, f32[1,2,720,256]{3,2,1,0:T(8,128)}, bf16[32,2,720,256]{3,2,1,0:T(8,128)(2,1)}, f32[1,2,720,256]{3,2,1,0:T(8,128)S(1)}, /*index=5*/s32[]{:T(128)}, s32[]{:T(128)}) while((s32[]{:T(128)}, f32[1,2,720,256]{3,2,1,0:T(8,128)}, f32[1,2,720,256]{3,2,1,0:T(8,128)}, ...), condition=%wide.region_1.2_spmd.clone, body=%wide.region_0.1_spmd.clone.sunk | while | flops 3317763 | bytes 8110179 | solution.py:74
  249.5 4.4 select_add_fusion.3
  253.9 4.4 select_add_fusion.3
  267.2 4.4 select_add_fusion.3
  280.4 4.4 select_add_fusion.3
  293.7 4.4 select_add_fusion.3
  302.5 4.4 select_add_fusion.3
  315.8 4.4 select_add_fusion.3
  329.0 4.4 select_add_fusion.3
  351.2 4.4 select_add_fusion.3
  364.4 4.4 select_add_fusion.3
  377.7 4.4 select_add_fusion.3
  399.8 5.7 fusion.12
  407.4 6.8 fusion.11
  414.2 6.8 fusion.10
  420.9 5.4 broadcast_in_dim.38
  426.3 8.8 %dynamic_update_slice.3 = f32[1,4,2880,256]{3,2,1,0:T(8,128)} dynamic-update-slice(f32[1,4,2880,256]{3,2,1,0:T(8,128)} %broadcast_in_dim.38, f32[1,4,752,256]{3,2,1,0:T(8,128)} %fusion.10, s32[]{:T(128)} %constant.322.clone.1, s32[]{:T(128)} %constant.322.clone.1, s32[]{:T(128)S(6)} %select_n.39, s32[]{:T(128)} %constant.322.clone.1) | dynamic-update-slice | bytes 6160388 | tf_op jit(solution)/shard_map/dynamic_update_slice | solution.py:174
  435.2 9.4 %fusion.3 = bf16[1,4,1440,256]{3,2,1,0:T(8,128)(2,1)} fusion(f32[1,4,2880,256]{3,2,1,0:T(8,128)} %dynamic_update_slice.3, f32[3,4,256]{2,0,1:T(4,128)S(1)} %fusion.41, f32[1,1440]{1,0:T(1,128)S(1)} %copy-done.11, f32[1,1440]{1,0:T(1,128)S(1)} %copy-done.13, f32[3]{0:T(128)S(1)} %copy-done.15), kind=kOutput, calls=%fused_computation.12 | convolution fusion | flops 57516480 | bytes 14769420 | tf_op jit(solution)/shard_map/pj,eprc->erjc/dot_general | solution.py:172
  445.7 6.4 convolution_bitcast_fusion.3
  452.8 73.8 %psum.15 = f32[]{:T(128)} all-reduce(f32[]{:T(128)S(6)} %div.141), channel_id=1, replica_groups=mesh['lat'=4,'lon'=2,'ens'=32] {'lat','lon','ens'}, use_global_device_ids=true, to_apply=%region_8.9 | all-reduce | flops 1 | bytes 8 | tf_op jit(solution)/shard_map/psum | solution.py:132
  533.8 195.4 %all-reduce.4.cloned.1.call-done = f32[9,256,256]{2,1,0:T(8,128)} async-done(((f32[9,256,256]{2,1,0:T(8,128)}), f32[9,256,256]{2,1,0:T(8,128)}) %all-reduce.4.cloned.1.call-update) | async-done | bytes 2359312 | tf_op jit(solution)/shard_map/psum | solution.py:132
  (157 shorter events, 158.5 us)
Async XLA Ops:
  7.2 60.0 %copy-start = (bf16[9,256,256]{2,1,0:T(8,128)(2,1)S(1)}, bf16[9,256,256]{2,1,0:T(8,128)(2,1)}, u32[]{:S(2)}) copy-start(bf16[9,256,256]{2,1,0:T(8,128)(2,1)} %param.23) | copy-start | bytes 3538948
  7.2 19.3 %copy-start.16 = (s32[2]{0:T(128)S(1)}, s32[2]{0:T(128)}, u32[]{:S(2)}) copy-start(s32[2]{0:T(128)} %param.24) | copy-start | bytes 28
  7.2 39.1 %all-gather.4.cloned.1.call-start = ((), (), s32[]{:S(2)}) async-start(), calls=%async_computation.1 | async-start | bytes 4423680 | tf_op jit(solution)/shard_map/all_gather | solution.py:96
  8.5 12.2 %collective-permute-start = (bf16[1,1,720,256]{3,2,1,0:T(8,128)(2,1)S(1)}, bf16[1,1,720,256]{3,2,1,0:T(8,128)(2,1)S(1)}, u32[]{:S(2)}, u32[]{:S(2)}) collective-permute-start(bf16[1,1,720,256]{3,2,1,0:T(8,128)(2,1)S(1)} %get-tuple-element.236), channel_id=1, source_target_pairs={{0,64},{64,128},{128,192},{1,65},{65,129},{129,193},{2,66},{66,130... | collective-permute-start | bytes 1105928 | tf_op jit(solution)/shard_map/ppermute | solution.py:17
  11.9 11.9 %collective-permute-start.1 = (bf16[1,1,720,256]{3,2,1,0:T(8,128)(2,1)S(1)}, bf16[1,1,720,256]{3,2,1,0:T(8,128)(2,1)S(1)}, u32[]{:S(2)}, u32[]{:S(2)}) collective-permute-start(bf16[1,1,720,256]{3,2,1,0:T(8,128)(2,1)S(1)} %get-tuple-element.237), channel_id=1, source_target_pairs={{64,0},{128,64},{192,128},{65,1},{129,65},{193,129},{66,2},{130,66... | collective-permute-start | bytes 1105928 | tf_op jit(solution)/shard_map/ppermute | solution.py:20
  26.3 219.6 %all-gather.6.cloned.1.call-start = ((), (), s32[]{:S(2)}) async-start(), calls=%async_computation.4 | async-start | bytes 24330240 | tf_op jit(solution)/shard_map/all_gather | solution.py:123
  26.4 25.0 %copy-start.14 = (f32[3]{0:T(128)}, f32[3]{0:T(128)S(1)}, u32[]{:S(2)}) copy-start(f32[3]{0:T(128)S(1)} %pad.37.clone) | copy-start | bytes 40
  26.7 24.6 %copy-start.10 = (f32[1,1440]{1,0:T(1,128)}, f32[1,1440]{1,0:T(1,128)S(1)}, u32[]{:S(2)}) copy-start(f32[1,1440]{1,0:T(1,128)S(1)} %get-tuple-element.247) | copy-start | bytes 17284
  26.7 24.6 %copy-start.12 = (f32[1,1440]{1,0:T(1,128)}, f32[1,1440]{1,0:T(1,128)S(1)}, u32[]{:S(2)}) copy-start(f32[1,1440]{1,0:T(1,128)S(1)} %get-tuple-element.248) | copy-start | bytes 17284
  27.0 30.9 %copy-start.6 = (f32[720,752]{1,0:T(8,128)}, f32[720,752]{1,0:T(8,128)S(1)}, u32[]{:S(2)}) copy-start(f32[720,752]{1,0:T(8,128)S(1)} %subtract_convert_fusion) | copy-start | bytes 6497284
  46.2 3.3 copy-start.2
  64.3 2.8 copy-start.4
  69.9 456.7 %reduce-scatter.2.cloned.1.call-start = ((), (), s32[]{:S(2)}) async-start(), calls=%async_computation.2 | async-start | bytes 4423680 | tf_op jit(solution)/shard_map/reduce_scatter | solution.py:176
  245.9 140.6 %copy-start.5 = (bf16[2,720,256]{2,1,0:T(8,128)(2,1)S(1)}, bf16[2,720,256]{2,1,0:T(8,128)(2,1)}, u32[]{:S(2)}) copy-start(bf16[2,720,256]{2,1,0:T(8,128)(2,1)} %bitcast_convert_fusion) | copy-start | bytes 2211844
  390.4 3.9 copy-start.8
  397.1 2.7 copy-start.7
  426.3 8.8 %copy-start.11 = (f32[1,1440]{1,0:T(1,128)S(1)}, f32[1,1440]{1,0:T(1,128)}, u32[]{:S(2)}) copy-start(f32[1,1440]{1,0:T(1,128)} %copy-done.10) | copy-start | bytes 17284
  426.3 8.8 %copy-start.13 = (f32[1,1440]{1,0:T(1,128)S(1)}, f32[1,1440]{1,0:T(1,128)}, u32[]{:S(2)}) copy-start(f32[1,1440]{1,0:T(1,128)} %copy-done.12) | copy-start | bytes 17284
  426.3 8.8 %copy-start.15 = (f32[3]{0:T(128)S(1)}, f32[3]{0:T(128)}, u32[]{:S(2)}) copy-start(f32[3]{0:T(128)} %copy-done.14) | copy-start | bytes 40
  444.6 284.5 %all-reduce.4.cloned.1.call-start = ((), (), s32[]{:S(2)}) async-start(), calls=%async_computation.3 | async-start | bytes 4718592 | tf_op jit(solution)/shard_map/psum | solution.py:132
  526.6 205.8 %copy-start.3 = (bf16[1,4,720,256]{3,2,1,0:T(8,128)(2,1)S(1)}, bf16[1,4,720,256]{3,2,1,0:T(8,128)(2,1)}, u32[]{:S(2)}) copy-start(bf16[1,4,720,256]{3,2,1,0:T(8,128)(2,1)} %reduce-scatter.2.cloned.1.call-done) | copy-start | bytes 4423684
  527.9 205.0 %collective-permute-start.2 = (bf16[1,1,720,256]{3,2,1,0:T(8,128)(2,1)S(1)}, bf16[1,1,720,256]{3,2,1,0:T(8,128)(2,1)S(1)}, u32[]{:S(2)}, u32[]{:S(2)}) collective-permute-start(bf16[1,1,720,256]{3,2,1,0:T(8,128)(2,1)S(1)} %get-tuple-element.234), channel_id=1, source_target_pairs={{0,64},{64,128},{128,192},{1,65},{65,129},{129,193},{2,66},{66,130... | collective-permute-start | bytes 1105928 | tf_op jit(solution)/shard_map/ppermute | solution.py:17
  530.8 202.0 %collective-permute-start.3 = (bf16[1,1,720,256]{3,2,1,0:T(8,128)(2,1)S(1)}, bf16[1,1,720,256]{3,2,1,0:T(8,128)(2,1)S(1)}, u32[]{:S(2)}, u32[]{:S(2)}) collective-permute-start(bf16[1,1,720,256]{3,2,1,0:T(8,128)(2,1)S(1)} %get-tuple-element.235), channel_id=1, source_target_pairs={{64,0},{128,64},{192,128},{65,1},{129,65},{193,129},{66,2},{130,66... | collective-permute-start | bytes 1105928 | tf_op jit(solution)/shard_map/ppermute | solution.py:20
  732.9 1.3 copy-start.1
  (1 other events, 1.1 us)
Sparse Core Ops, SparseCore 0:
  26.4 19.8 all-gather.3
  70.1 175.7 all-gather.5
  444.7 13.3 reduce-scatter.1
  464.0 265.1 all-reduce.3
where the time goes:
time: 742 us; the launch traced here: 741 us
  waiting for transfers between devices  399 us (54%)
  other arithmetic  159 us (21%)
  blocking collectives  73.8 us (10%)
  matrix products  59.5 us (8%)
  local copies, waits for them, and re-layouts  23.1 us (3%)
  between operations  15.1 us (2%)
  starting transfers between devices  12.1 us (2%)
    psum x1, waiting for transfers between devices, per_device(): weight_sum, loss = lax.psum((weight_part, loss_part), ('lat', 'lon', 'ens'))  195 us
    all_gather x1, waiting for transfers between devices, per_device(): ensemble = lax.all_gather(response, 'ens', axis=0, tiled=True)  174 us
    add x32, other arithmetic, add_member(): return (pair_dist + distance, pair_slope + gap_value / distance)  141 us
    psum x1, blocking collectives, per_device(): weight_sum, loss = lax.psum((weight_part, loss_part), ('lat', 'lon', 'ens'))  73.8 us
    all_gather x1, waiting for transfers between devices, per_device(): whole_circle = lax.all_gather(extended, 'lon', axis=2, tiled=True)  19.3 us
    dot_general x3, matrix products, per_device(): jnp.einsum('objq,eobjc->eoqc', kernels, picked, preferred_element_type=jn...  19.3 us
  transfers between devices with their start and end apart: 8, of which 5 were waited for; matrix products, arithmetic and copies ran while one was open for 2% of the time, Pallas kernels for 0%

commit v1 on v0

--- a/solution.py
+++ b/solution.py
@@ -129,7 +129,7 @@
     weight_part = jnp.einsum(
         "eokjc,eojd->kcd", features, slopes, preferred_element_type=jnp.float32
     )
-    weight_sum, loss = lax.psum((weight_part, loss_part), ("lat", "lon", "ens"))
+    weight_sum, loss = lax.psum(lax.psum((weight_part, loss_part), ("lon", "ens")), "lat")
     grad_weight = weight_sum * math.sqrt(weight.shape[0] * channels) / (lat_total * lon_total)
     feature_grad = jnp.einsum(
         "eojd,kcd->eokjc", slopes, weight, preferred_element_type=jnp.float32

time: 742 us -> 766 us (1.032); the launches traced: 741 us -> 755 us
  blocking collectives: 73.8 us -> 137 us
  waiting for transfers between devices: 399 us -> 349 us
    psum x1 -> x2, blocking collectives: 73.8 us -> 137 us  [the longest x1 128 us: per_device(): lax.psum((weight_part, loss_part), ('lon', 'ens'))]
    psum x1 -> x2, waiting for transfers between devices: 195 us -> 143 us  [the longest x1 143 us: per_device(): lax.psum((weight_part, loss_part), ('lon', 'ens'))]
  transfers between devices with their start and end apart: 8 -> 9, of which waited for: 5 -> 6; matrix products, arithmetic and copies ran while one was open for 2% -> 7% of each run, Pallas kernels for 0% -> 0%
where the time goes in v1:
time: 766 us; the launch traced here: 755 us
  waiting for transfers between devices  349 us (46%)
  other arithmetic  160 us (21%)
  blocking collectives  137 us (18%)
  matrix products  59.6 us (8%)
  local copies, waits for them, and re-layouts  22.2 us (3%)
  between operations  15.1 us (2%)
  starting transfers between devices  12.3 us (2%)
    all_gather x1, waiting for transfers between devices, per_device(): ensemble = lax.all_gather(response, 'ens', axis=0, tiled=True)  174 us
    psum x1, waiting for transfers between devices, per_device(): lax.psum((weight_part, loss_part), ('lon', 'ens'))  143 us
    add x32, other arithmetic, add_member(): return (pair_dist + distance, pair_slope + gap_value / distance)  142 us
    psum x1, blocking collectives, per_device(): lax.psum((weight_part, loss_part), ('lon', 'ens'))  128 us
    dot_general x3, matrix products, per_device(): jnp.einsum('objq,eobjc->eoqc', kernels, picked, preferred_element_type=jn...  19.3 us
    all_gather x1, waiting for transfers between devices, per_device(): whole_circle = lax.all_gather(extended, 'lon', axis=2, tiled=True)  19.3 us
  transfers between devices with their start and end apart: 9, of which 6 were waited for; matrix products, arithmetic and copies ran while one was open for 7% of the time, Pallas kernels for 0%

profile of v1, /device:TPU:2, one launch (start us, length us, event | category | flops | bytes accessed | tf_op | source)
XLA Modules:
  0.0 755.4 jit_solution(6883092710609126620)
XLA Ops:
  14.4 6.3 collective-permute-done
  27.0 19.3 %all-gather.4.cloned.1.call-done = bf16[1,4,1440,256]{3,2,1,0:T(8,128)(2,1)} async-done(((bf16[1,4,720,256]{3,2,1,0:T(8,128)(2,1)}), bf16[1,4,1440,256]{3,2,1,0:T(8,128)(2,1)}) %all-gather.4.cloned.1.call-update) | async-done | bytes 2949136 | tf_op jit(solution)/shard_map/all_gather | solution.py:96
  71.4 174.4 %all-gather.6.cloned.1.call-done = bf16[64,720,256]{2,1,0:T(8,128)(2,1)} async-done(((bf16[2,720,256]{2,1,0:T(8,128)(2,1)}), bf16[64,720,256]{2,1,0:T(8,128)(2,1)}) %all-gather.6.cloned.1.call-update) | async-done | bytes 23592976 | tf_op jit(solution)/shard_map/all_gather | solution.py:123
  245.8 142.3 %while.24 = (s32[]{:T(128)}, f32[1,2,720,256]{3,2,1,0:T(8,128)}, f32[1,2,720,256]{3,2,1,0:T(8,128)}, bf16[32,2,720,256]{3,2,1,0:T(8,128)(2,1)}, f32[1,2,720,256]{3,2,1,0:T(8,128)S(1)}, /*index=5*/s32[]{:T(128)}, s32[]{:T(128)}) while((s32[]{:T(128)}, f32[1,2,720,256]{3,2,1,0:T(8,128)}, f32[1,2,720,256]{3,2,1,0:T(8,128)}, ...), condition=%wide.region_1.2_spmd.clone, body=%wide.region_0.1_spmd.clone.sunk | while | flops 3317763 | bytes 8110179 | solution.py:74
  249.5 4.5 select_add_fusion.3
  253.9 4.5 select_add_fusion.3
  262.9 4.5 select_add_fusion.3
  267.4 4.5 select_add_fusion.3
  271.8 4.5 select_add_fusion.3
  276.3 4.5 select_add_fusion.3
  280.8 4.5 select_add_fusion.3
  285.3 4.5 select_add_fusion.3
  289.7 4.5 select_add_fusion.3
  294.2 4.5 select_add_fusion.3
  392.1 6.4 convolution_bitcast_fusion.3
  408.0 5.7 fusion.12
  415.5 6.8 fusion.11
  422.3 6.8 fusion.10
  429.4 5.4 broadcast_in_dim.38
  434.8 8.8 %dynamic_update_slice.3 = f32[1,4,2880,256]{3,2,1,0:T(8,128)} dynamic-update-slice(f32[1,4,2880,256]{3,2,1,0:T(8,128)} %broadcast_in_dim.38, f32[1,4,752,256]{3,2,1,0:T(8,128)} %fusion.10, s32[]{:T(128)} %constant.322.clone.1, s32[]{:T(128)} %constant.322.clone.1, s32[]{:T(128)S(6)} %select_n.39, s32[]{:T(128)} %constant.322.clone.1) | dynamic-update-slice | bytes 6160388 | tf_op jit(solution)/shard_map/dynamic_update_slice | solution.py:174
  443.6 9.5 %fusion.3 = bf16[1,4,1440,256]{3,2,1,0:T(8,128)(2,1)} fusion(f32[1,4,2880,256]{3,2,1,0:T(8,128)} %dynamic_update_slice.3, f32[3,4,256]{2,0,1:T(4,128)S(1)} %fusion.41, f32[1,1440]{1,0:T(1,128)S(1)} %copy-done.9, f32[1,1440]{1,0:T(1,128)S(1)} %copy-done.11, f32[3]{0:T(128)S(1)} %copy-done.13), kind=kOutput, calls=%fused_computation.12 | convolution fusion | flops 57516480 | bytes 14769420 | tf_op jit(solution)/shard_map/pj,eprc->erjc/dot_general | solution.py:172
  453.1 142.6 %all-reduce.5.cloned.1.call-done = f32[9,256,256]{2,1,0:T(8,128)} async-done(((f32[9,256,256]{2,1,0:T(8,128)}), f32[9,256,256]{2,1,0:T(8,128)}) %all-reduce.5.cloned.1.call-update) | async-done | bytes 2359312 | tf_op jit(solution)/shard_map/psum | solution.py:132
  596.4 128.1 %psum.30 = f32[]{:T(128)} all-reduce(f32[]{:T(128)S(6)} %div.141), channel_id=1, replica_groups=mesh['lat'=4,'lon'=2,'ens'=32] {'lon','ens'}, use_global_device_ids=true, to_apply=%region_9.10 | all-reduce | flops 1 | bytes 8 | tf_op jit(solution)/shard_map/psum | solution.py:132
  724.5 9.2 %psum.31 = f32[]{:T(128)} all-reduce(f32[]{:T(128)} %psum.30), channel_id=1, replica_groups=mesh['lat'=4,'lon'=2,'ens'=32] {'lat'}, use_global_device_ids=true, to_apply=%region_10.11 | all-reduce | flops 1 | bytes 8 | tf_op jit(solution)/shard_map/psum | solution.py:132
  (157 shorter events, 166.4 us)
Async XLA Ops:
  7.2 59.9 %copy-start = (bf16[9,256,256]{2,1,0:T(8,128)(2,1)S(1)}, bf16[9,256,256]{2,1,0:T(8,128)(2,1)}, u32[]{:S(2)}) copy-start(bf16[9,256,256]{2,1,0:T(8,128)(2,1)} %param.23) | copy-start | bytes 3538948
  7.2 19.2 %copy-start.14 = (s32[2]{0:T(128)S(1)}, s32[2]{0:T(128)}, u32[]{:S(2)}) copy-start(s32[2]{0:T(128)} %param.24) | copy-start | bytes 28
  7.2 39.0 %all-gather.4.cloned.1.call-start = ((), (), s32[]{:S(2)}) async-start(), calls=%async_computation.1 | async-start | bytes 4423680 | tf_op jit(solution)/shard_map/all_gather | solution.py:96
  8.5 12.2 %collective-permute-start = (bf16[1,1,720,256]{3,2,1,0:T(8,128)(2,1)S(1)}, bf16[1,1,720,256]{3,2,1,0:T(8,128)(2,1)S(1)}, u32[]{:S(2)}, u32[]{:S(2)}) collective-permute-start(bf16[1,1,720,256]{3,2,1,0:T(8,128)(2,1)S(1)} %get-tuple-element.236), channel_id=1, source_target_pairs={{0,64},{64,128},{128,192},{1,65},{65,129},{129,193},{2,66},{66,130... | collective-permute-start | bytes 1105928 | tf_op jit(solution)/shard_map/ppermute | solution.py:17
  11.9 11.9 %collective-permute-start.1 = (bf16[1,1,720,256]{3,2,1,0:T(8,128)(2,1)S(1)}, bf16[1,1,720,256]{3,2,1,0:T(8,128)(2,1)S(1)}, u32[]{:S(2)}, u32[]{:S(2)}) collective-permute-start(bf16[1,1,720,256]{3,2,1,0:T(8,128)(2,1)S(1)} %get-tuple-element.237), channel_id=1, source_target_pairs={{64,0},{128,64},{192,128},{65,1},{129,65},{193,129},{66,2},{130,66... | collective-permute-start | bytes 1105928 | tf_op jit(solution)/shard_map/ppermute | solution.py:20
  26.2 219.6 %all-gather.6.cloned.1.call-start = ((), (), s32[]{:S(2)}) async-start(), calls=%async_computation.5 | async-start | bytes 24330240 | tf_op jit(solution)/shard_map/all_gather | solution.py:123
  26.3 25.0 %copy-start.12 = (f32[3]{0:T(128)}, f32[3]{0:T(128)S(1)}, u32[]{:S(2)}) copy-start(f32[3]{0:T(128)S(1)} %pad.37.clone) | copy-start | bytes 40
  26.7 24.6 %copy-start.8 = (f32[1,1440]{1,0:T(1,128)}, f32[1,1440]{1,0:T(1,128)S(1)}, u32[]{:S(2)}) copy-start(f32[1,1440]{1,0:T(1,128)S(1)} %get-tuple-element.247) | copy-start | bytes 17284
  26.7 24.6 %copy-start.10 = (f32[1,1440]{1,0:T(1,128)}, f32[1,1440]{1,0:T(1,128)S(1)}, u32[]{:S(2)}) copy-start(f32[1,1440]{1,0:T(1,128)S(1)} %get-tuple-element.248) | copy-start | bytes 17284
  26.9 30.9 %copy-start.6 = (f32[720,752]{1,0:T(8,128)}, f32[720,752]{1,0:T(8,128)S(1)}, u32[]{:S(2)}) copy-start(f32[720,752]{1,0:T(8,128)S(1)} %subtract_convert_fusion) | copy-start | bytes 6497284
  46.2 3.3 copy-start.2
  64.3 2.8 copy-start.4
  69.9 525.9 %all-reduce.5.cloned.1.call-start = ((), (), s32[]{:S(2)}) async-start(), calls=%async_computation.3 | async-start | bytes 4718592 | tf_op jit(solution)/shard_map/psum | solution.py:132
  245.8 142.3 %copy-start.5 = (bf16[2,720,256]{2,1,0:T(8,128)(2,1)S(1)}, bf16[2,720,256]{2,1,0:T(8,128)(2,1)}, u32[]{:S(2)}) copy-start(bf16[2,720,256]{2,1,0:T(8,128)(2,1)} %bitcast_convert_fusion) | copy-start | bytes 2211844
  406.3 1.6 copy-start.7
  407.5 326.2 %reduce-scatter.2.cloned.1.call-start = ((), (), s32[]{:S(2)}) async-start(), calls=%async_computation.2 | async-start | bytes 4423680 | tf_op jit(solution)/shard_map/reduce_scatter | solution.py:176
  434.8 8.8 %copy-start.9 = (f32[1,1440]{1,0:T(1,128)S(1)}, f32[1,1440]{1,0:T(1,128)}, u32[]{:S(2)}) copy-start(f32[1,1440]{1,0:T(1,128)} %copy-done.8) | copy-start | bytes 17284
  434.8 8.8 %copy-start.11 = (f32[1,1440]{1,0:T(1,128)S(1)}, f32[1,1440]{1,0:T(1,128)}, u32[]{:S(2)}) copy-start(f32[1,1440]{1,0:T(1,128)} %copy-done.10) | copy-start | bytes 17284
  434.8 8.8 %copy-start.13 = (f32[3]{0:T(128)S(1)}, f32[3]{0:T(128)}, u32[]{:S(2)}) copy-start(f32[3]{0:T(128)} %copy-done.12) | copy-start | bytes 40
  453.1 287.8 %all-reduce.7.cloned.1.call-start = ((), (), s32[]{:S(2)}) async-start(), calls=%async_computation.4 | async-start | bytes 4718592 | tf_op jit(solution)/shard_map/psum | solution.py:132
  733.7 10.4 %copy-start.3 = (bf16[1,4,720,256]{3,2,1,0:T(8,128)(2,1)S(1)}, bf16[1,4,720,256]{3,2,1,0:T(8,128)(2,1)}, u32[]{:S(2)}) copy-start(bf16[1,4,720,256]{3,2,1,0:T(8,128)(2,1)} %reduce-scatter.2.cloned.1.call-done) | copy-start | bytes 4423684
  735.0 9.6 %collective-permute-start.2 = (bf16[1,1,720,256]{3,2,1,0:T(8,128)(2,1)S(1)}, bf16[1,1,720,256]{3,2,1,0:T(8,128)(2,1)S(1)}, u32[]{:S(2)}, u32[]{:S(2)}) collective-permute-start(bf16[1,1,720,256]{3,2,1,0:T(8,128)(2,1)S(1)} %get-tuple-element.234), channel_id=1, source_target_pairs={{0,64},{64,128},{128,192},{1,65},{65,129},{129,193},{2,66},{66,130... | collective-permute-start | bytes 1105928 | tf_op jit(solution)/shard_map/ppermute | solution.py:17
  738.1 9.4 %collective-permute-start.3 = (bf16[1,1,720,256]{3,2,1,0:T(8,128)(2,1)S(1)}, bf16[1,1,720,256]{3,2,1,0:T(8,128)(2,1)S(1)}, u32[]{:S(2)}, u32[]{:S(2)}) collective-permute-start(bf16[1,1,720,256]{3,2,1,0:T(8,128)(2,1)S(1)} %get-tuple-element.235), channel_id=1, source_target_pairs={{64,0},{128,64},{192,128},{65,1},{129,65},{193,129},{66,2},{130,66... | collective-permute-start | bytes 1105928 | tf_op jit(solution)/shard_map/ppermute | solution.py:20
  747.5 1.4 copy-start.1
Sparse Core Ops, SparseCore 0:
  26.4 19.8 all-gather.3
  70.0 175.7 all-gather.5
  407.6 188.1 all-reduce.4
  598.1 15.0 reduce-scatter.1
  615.4 68.1 all-reduce.6
